TPU v7x, 128 devices: a whole 4x4x4 slice. The times are simulated.
128 devices in a mesh: grp: 8 (over y_lo, z), dev: 16 (over y_hi, x, core).
Axes of the slice: x: 4, y: 4 (y_hi: 2, y_lo: 2; y = y_hi * 2 + y_lo), z: 4, core: 2. Of those that a mesh axis runs over, the one named last changes fastest.
Arguments:
- queries: bfloat16 [131072, 2048], P(('grp', 'dev')), may hold values from -48 to 48
- key_rows: bfloat16 [131072, 2048], P(('grp', 'dev')), may hold values from -6 to 6
- value_rows: bfloat16 [131072, 2048], P(('grp', 'dev')), may hold values from -6 to 6
Outputs:
- attended: bfloat16 [131072, 2048], P(('grp', 'dev'))
All inputs are finite; a program needn't handle non-finite values.
Results may differ from a plain program's by a relative error of at most 0.0026.
Values may be sent and summed in bfloat16 or wider, within the bound.
A program may use at most 256 MiB of HBM per device.

v0:
```python
import math
import jax
import jax.numpy as jnp
import numpy as np
from jax import lax
from jax.sharding import PartitionSpec as P

H = 16


def attend(query_rows, key_part, value_part):
    score_scale = 1.0 / math.sqrt(query_rows.shape[-1])
    scores = (
        jnp.einsum("qhe,khe->hqk", query_rows, key_part, preferred_element_type=jnp.float32)
        * score_scale
    )
    maxima = jnp.max(scores, axis=2)
    weights = jnp.exp(scores - maxima[:, :, None])
    totals = jnp.sum(weights, axis=2)
    summed = jnp.einsum(
        "hqk,khe->qhe", weights.astype(jnp.bfloat16), value_part, preferred_element_type=jnp.float32
    )
    return (maxima.T, totals.T, summed)


def start_state(query_rows):
    row_count, head_count, head_width = query_rows.shape
    return (
        jnp.full((row_count, head_count), -jnp.inf, jnp.float32),
        jnp.zeros((row_count, head_count), jnp.float32),
        jnp.zeros((row_count, head_count, head_width), jnp.float32),
    )


def folder(query_rows, state_now, shard_piece):
    score_scale = 1.0 / math.sqrt(query_rows.shape[-1])
    maxima, totals, summed = state_now
    key_part, value_part = shard_piece
    scores = (
        jnp.einsum("qhe,khe->hqk", query_rows, key_part, preferred_element_type=jnp.float32)
        * score_scale
    )
    raised = jnp.maximum(maxima, jnp.max(scores, axis=2).T)
    weights = jnp.exp(scores - raised.T[:, :, None])
    shrink = jnp.exp(maxima - raised)
    totals = totals * shrink + jnp.sum(weights, axis=2).T
    summed = summed * shrink[:, :, None] + jnp.einsum(
        "hqk,khe->qhe", weights.astype(jnp.bfloat16), value_part, preferred_element_type=jnp.float32
    )
    return (raised, totals, summed)


def picked_rows(source, dilation):
    head_ids = np.arange(source.shape[1])
    shaped = source.reshape(source.shape[0] // dilation, dilation, source.shape[1], source.shape[2])
    return shaped[:, head_ids % dilation, head_ids, :]


def gap_between(maxima, totals, summed, dilation):
    head_count = maxima.shape[1]
    select_mask = jnp.asarray(
        np.arange(dilation)[:, None] == (np.arange(head_count) % dilation)[None, :]
    )
    full_max = jnp.where(select_mask[None], maxima[:, None, :], -jnp.inf).reshape(-1, head_count)
    full_tot = jnp.where(select_mask[None], totals[:, None, :], 0.0).reshape(-1, head_count)
    full_sum = jnp.where(select_mask[None, :, :, None], summed[:, None], 0.0).reshape(
        -1, head_count, summed.shape[2]
    )
    return (full_max, full_tot, full_sum)


def combine(branch_list):
    highest = branch_list[0][0]
    for branch in branch_list[1:]:
        highest = jnp.maximum(highest, branch[0])
    numerator = jnp.zeros_like(branch_list[0][2])
    denominator = jnp.zeros_like(branch_list[0][1])
    for branch in branch_list:
        factor = jnp.exp(branch[0] - highest)
        denominator = denominator + branch[1] * factor
        numerator = numerator + branch[2] * factor[:, :, None]
    return numerator / denominator[:, :, None]


def body(queries, key_rows, value_rows):
    tok_rows = queries.shape[0]
    head_width = queries.shape[1] // H
    processor_count = lax.axis_size("dev")
    group_number = lax.axis_size("grp")
    global_dilation = processor_count * group_number
    query_per_head = queries.reshape(tok_rows, H, head_width)
    key_per_head = key_rows.reshape(tok_rows, H, head_width)
    value_per_head = value_rows.reshape(tok_rows, H, head_width)
    block_rows = min(512, tok_rows)
    query_blocks = query_per_head.reshape(tok_rows // block_rows, block_rows, H, head_width)
    local_max, local_tot, local_sum = lax.map(
        lambda chosen: attend(chosen, key_per_head, value_per_head), query_blocks
    )
    local_part = (
        local_max.reshape(tok_rows, H),
        local_tot.reshape(tok_rows, H),
        local_sum.reshape(tok_rows, H, head_width),
    )
    group_query = picked_rows(query_per_head, processor_count)
    group_key = picked_rows(key_per_head, processor_count)
    group_value = picked_rows(value_per_head, processor_count)
    global_query = picked_rows(query_per_head, global_dilation)
    global_key = picked_rows(key_per_head, global_dilation)
    global_value = picked_rows(value_per_head, global_dilation)
    global_portion = folder(
        global_query,
        start_state(global_query),
        (
            lax.all_gather(global_key, ("grp", "dev"), axis=0, tiled=True),
            lax.all_gather(global_value, ("grp", "dev"), axis=0, tiled=True),
        ),
    )
    group_portion = folder(
        group_query,
        start_state(group_query),
        (
            lax.all_gather(group_key, "dev", axis=0, tiled=True),
            lax.all_gather(group_value, "dev", axis=0, tiled=True),
        ),
    )
    result = combine(
        [
            local_part,
            gap_between(group_portion[0], group_portion[1], group_portion[2], processor_count),
            gap_between(global_portion[0], global_portion[1], global_portion[2], global_dilation),
        ]
    )
    return result.reshape(tok_rows, H * head_width).astype(jnp.bfloat16)


def solution(mesh):
    in_specs = (P(("grp", "dev"), None), P(("grp", "dev"), None), P(("grp", "dev"), None))
    out_specs = P(("grp", "dev"), None)
    return jax.shard_map(body, mesh=mesh, in_specs=in_specs, out_specs=out_specs, check_vma=False)
```

profile of v0, /device:TPU:1, one launch (start us, length us, event | category | flops | bytes accessed | tf_op | source)
XLA Modules:
  0.0 651.3 jit_solution(3880444532441547648)
XLA Ops:
  6.5 3.6 copy.88
  10.2 2.0 copy-done.3
  12.2 4.7 copy.61
  16.8 3.5 gather_fusion.1
  20.4 3.6 copy.95
  24.0 2.0 copy-done.2
  25.9 4.7 copy.66
  30.6 3.5 gather_fusion.4
  34.4 9.0 %copy.63 = bf16[8,128,16,128]{3,0,2,1:T(8,128)(2,1)} copy(bf16[8,128,16,128]{3,2,1,0:T(8,128)(2,1)} %bitcast.202) | data formatting | bytes 8388608 | tf_op jit(solution)/shard_map/reshape;reshape | solution.py:55
  43.4 3.4 gather_fusion.3
  47.1 9.1 %copy.70 = bf16[8,128,16,128]{3,0,2,1:T(8,128)(2,1)} copy(bf16[8,128,16,128]{3,2,1,0:T(8,128)(2,1)} %bitcast.200) | data formatting | bytes 8388608 | tf_op jit(solution)/shard_map/reshape;reshape | solution.py:55
  56.2 3.4 gather_fusion.5
  59.6 6.4 copy.53
  66.1 6.4 copy.54
  72.5 5.6 copy.84
  78.1 6.4 copy.56
  84.5 6.4 copy.57
  90.9 115.2 %while.14 = (s32[]{:T(128)}, f32[2,512,16]{1,0,2:T(2,128)S(1)}, f32[2,512,16]{1,0,2:T(2,128)S(1)}, f32[2,512,16,128]{3,2,1,0:T(8,128)}, bf16[2,512,16,128]{3,2,1...) while((s32[]{:T(128)}, f32[2,512,16]{1,0,2:T(2,128)S(1)}, ...), condition=%wide.region_3.4_spmd, body=%wide.region_0.3_spmd.sunk | while | flops 4362059776 | bytes 145096848 | solution.py:96
  91.3 3.5 constant_dynamic-slice_fusion.2
  94.8 14.8 %multiply_reduce_fusion.3 = (f32[16,512]{1,0:T(8,128)S(1)}, f32[16,512,1024]{2,1,0:T(8,128)}) fusion(bf16[1024,16,128]{2,0,1:T(8,128)(2,1)S(1)} %copy-done, bf16[1,512,16,128]{3,2,1,0:T(8,128)(2,1)} %constant_dynamic-slice_fusion.2), kind=kOutput, calls=%fused_computation.7.clone.1 | convolution fusion | flops 2164252672 | bytes 39878656 | tf_op jit(solution)/shard_map/while/body/eval_jaxpr/qhe,khe->hqk/dot_general | solution.py:14
  109.8 14.4 %fusion.60 = f32[16,512]{1,0:T(8,128)S(1)} fusion(f32[16,512,1024]{2,1,0:T(8,128)} %get-tuple-element.135, f32[16,512]{1,0:T(8,128)S(1)} %get-tuple-element.134), kind=kLoop, calls=%fused_computation.9.clone.1 | loop fusion | flops 25157632 | bytes 33619968 | tf_op jit(solution)/shard_map/while/body/eval_jaxpr/reduce_sum | solution.py:19
  124.5 17.8 %fusion.61 = f32[1,512,16,128]{3,1,2,0:T(8,128)} fusion(bf16[1024,16,128]{2,0,1:T(8,128)(2,1)} %get-tuple-element.160, f32[16,512,1024]{2,1,0:T(8,128)} %get-tuple-element.135, f32[16,512]{1,0:T(8,128)S(1)} %get-tuple-element.134), kind=kOutput, calls=%fused_computation.14.clone.1 | convolution fusion | flops 2172649472 | bytes 41975808 | tf_op jit(solution)/shard_map/while/body/eval_jaxpr/hqk,khe->qhe/dot_general | solution.py:20
  142.3 6.7 %copy_dynamic-update-slice_fusion.2 = f32[2,512,16,128]{3,2,1,0:T(8,128)} fusion(f32[2,512,16,128]{3,2,1,0:T(8,128)} %get-tuple-element.148, s32[]{:T(128)S(6)} %copy.162, f32[1,512,16,128]{3,1,2,0:T(8,128)} %fusion.61), kind=kLoop, calls=%fused_computation.13.clone.1 | loop fusion | bytes 8388612 | tf_op jit(solution)/shard_map/while/body/jit(dynamic_update_index_in_dim)/dynamic_update_slice | solution.py:96
  149.0 3.4 constant_dynamic-slice_fusion.2
  152.4 14.8 %multiply_reduce_fusion.3 = (f32[16,512]{1,0:T(8,128)S(1)}, f32[16,512,1024]{2,1,0:T(8,128)}) fusion(bf16[1024,16,128]{2,0,1:T(8,128)(2,1)S(1)} %copy-done, bf16[1,512,16,128]{3,2,1,0:T(8,128)(2,1)} %constant_dynamic-slice_fusion.2), kind=kOutput, calls=%fused_computation.7.clone.1 | convolution fusion | flops 2164252672 | bytes 39878656 | tf_op jit(solution)/shard_map/while/body/eval_jaxpr/qhe,khe->hqk/dot_general | solution.py:14
  167.4 14.3 %fusion.60 = f32[16,512]{1,0:T(8,128)S(1)} fusion(f32[16,512,1024]{2,1,0:T(8,128)} %get-tuple-element.135, f32[16,512]{1,0:T(8,128)S(1)} %get-tuple-element.134), kind=kLoop, calls=%fused_computation.9.clone.1 | loop fusion | flops 25157632 | bytes 33619968 | tf_op jit(solution)/shard_map/while/body/eval_jaxpr/reduce_sum | solution.py:19
  182.0 17.4 %fusion.61 = f32[1,512,16,128]{3,1,2,0:T(8,128)} fusion(bf16[1024,16,128]{2,0,1:T(8,128)(2,1)} %get-tuple-element.160, f32[16,512,1024]{2,1,0:T(8,128)} %get-tuple-element.135, f32[16,512]{1,0:T(8,128)S(1)} %get-tuple-element.134), kind=kOutput, calls=%fused_computation.14.clone.1 | convolution fusion | flops 2172649472 | bytes 41975808 | tf_op jit(solution)/shard_map/while/body/eval_jaxpr/hqk,khe->qhe/dot_general | solution.py:20
  199.4 6.6 %copy_dynamic-update-slice_fusion.2 = f32[2,512,16,128]{3,2,1,0:T(8,128)} fusion(f32[2,512,16,128]{3,2,1,0:T(8,128)} %get-tuple-element.148, s32[]{:T(128)S(6)} %copy.162, f32[1,512,16,128]{3,1,2,0:T(8,128)} %fusion.61), kind=kLoop, calls=%fused_computation.13.clone.1 | loop fusion | bytes 8388612 | tf_op jit(solution)/shard_map/while/body/jit(dynamic_update_index_in_dim)/dynamic_update_slice | solution.py:96
  206.1 9.0 %copy.62 = bf16[8,128,16,128]{3,0,2,1:T(8,128)(2,1)} copy(bf16[8,128,16,128]{3,2,1,0:T(8,128)(2,1)} %bitcast.197) | data formatting | bytes 8388608 | tf_op jit(solution)/shard_map/reshape;reshape | solution.py:55
  215.2 2.8 gather_fusion.2
  218.4 6.9 %copy.60 = bf16[64,16,16,128]{3,0,2,1:T(8,128)(2,1)} copy(bf16[64,16,16,128]{3,2,1,0:T(8,128)(2,1)} %bitcast.198) | data formatting | bytes 8388608 | tf_op jit(solution)/shard_map/reshape;reshape | solution.py:55
  225.2 2.8 gather_fusion
  228.7 3.9 multiply_reduce_fusion.1
  232.5 2.0 copy-done.1
  236.4 4.8 fusion.23
  241.6 102.9 %all-gather.7.cloned.1.call-done = bf16[1024,16,128]{2,0,1:T(8,128)(2,1)} async-done(((bf16[8,16,128]{2,0,1:T(8,128)(2,1)}), bf16[1024,16,128]{2,0,1:T(8,128)(2,1)}) %all-gather.7.cloned.1.call-update) | async-done | bytes 4194320 | tf_op jit(solution)/shard_map/all_gather | solution.py:114
  344.5 3.4 fusion.45
  348.9 201.5 %all-gather.11.cloned.1.call-done = bf16[1024,16,128]{2,0,1:T(8,128)(2,1)} async-done(((bf16[8,16,128]{2,0,1:T(8,128)(2,1)}), bf16[1024,16,128]{2,0,1:T(8,128)(2,1)}) %all-gather.11.cloned.1.call-update) | async-done | bytes 4194320 | tf_op jit(solution)/shard_map/all_gather | solution.py:115
  550.4 2.9 fusion.26
  553.7 5.9 div.11
  559.7 6.0 mul.91
  565.7 3.8 broadcast_in_dim.234
  569.5 6.0 mul.87
  575.5 3.9 broadcast_in_dim.225
  579.4 5.8 mul.83
  585.2 6.9 %broadcast_in_dim.228 = pred[1024,16,128]{2,1,0:T(8,128)(4,1)S(1)} broadcast(pred[1024,16]{1,0:T(8,128)(4,1)S(1)} %copy.69), dimensions={0,1} | broadcast | bytes 2113536 | tf_op jit(solution)/shard_map/jit(_where)/broadcast_in_dim | solution.py:66
  592.1 6.9 %broadcast_in_dim.219 = pred[1024,16,128]{2,1,0:T(8,128)(4,1)S(1)} broadcast(pred[1024,16]{1,0:T(8,128)(4,1)S(1)} %copy.65), dimensions={0,1} | broadcast | bytes 2113536 | tf_op jit(solution)/shard_map/jit(_where)/broadcast_in_dim | solution.py:66
  599.0 45.3 %fusion.11 = bf16[1024,2048]{1,0:T(8,128)(2,1)} fusion(f32[128,8,16,128]{3,2,1,0:T(8,128)} %bitcast.203, f32[128,8,16,128]{3,2,1,0:T(8,128)} %bitcast.204, f32[128,8,16,128]{3,2,1,0:T(8,128)} %bitcast.205, f32[128,8,16,128]{3,2,1,0:T(8,128)} %bitcast.206, f32[128,8,16,128]{3,2,1,0:T(8,128)} %bitcast.207, f32[128,8,16,128]{3,2,1,0:T(8,128)} %bitcast.208, ...), kind=kLoop, calls=%fused_computation.20 | loop fusion | flops 18874368 | bytes 67108864 | tf_op jit(solution)/shard_map/convert_element_type | solution.py:133
  (67 shorter events, 5.9 us)
Async XLA Ops:
  6.5 222.2 %all-gather.5.cloned.1.call-start = ((), (), s32[]{:S(2)}) async-start(), calls=%async_computation | async-start | bytes 4456448 | tf_op jit(solution)/shard_map/all_gather | solution.py:122
  6.5 24.1 %copy-start.4 = (s32[16]{0:T(128)}, s32[16]{0:T(128)S(1)}, u32[]{:S(2)}) copy-start(s32[16]{0:T(128)S(1)} %fusion.40) | copy-start | bytes 196
  10.1 2.0 copy-start.3
  20.3 216.1 %all-gather.9.cloned.1.call-start = ((), (), s32[]{:S(2)}) async-start(), calls=%async_computation.2 | async-start | bytes 4456448 | tf_op jit(solution)/shard_map/all_gather | solution.py:123
  24.0 2.0 copy-start.2
  34.1 310.4 %all-gather.7.cloned.1.call-start = ((), (), s32[]{:S(2)}) async-start(), calls=%async_computation.1 | async-start | bytes 4227072 | tf_op jit(solution)/shard_map/all_gather | solution.py:114
  43.4 12.8 %copy-start.6 = (s32[16]{0:T(128)}, s32[16]{0:T(128)S(1)}, u32[]{:S(2)}) copy-start(s32[16]{0:T(128)S(1)} %fusion.42) | copy-start | bytes 196
  46.8 503.6 %all-gather.11.cloned.1.call-start = ((), (), s32[]{:S(2)}) async-start(), calls=%async_computation.3 | async-start | bytes 4227072 | tf_op jit(solution)/shard_map/all_gather | solution.py:115
  91.3 3.5 copy-start
  149.0 3.5 copy-start
  206.1 9.1 %copy-start.7 = (s32[16]{0:T(128)S(1)}, s32[16]{0:T(128)}, u32[]{:S(2)}) copy-start(s32[16]{0:T(128)} %copy-done.6) | copy-start | bytes 196
  206.1 11.9 %copy-start.8 = (pred[16,16]{0,1:T(8,128)(4,1)S(1)}, pred[16,16]{0,1:T(8,128)(4,1)}, u32[]{:S(2)}) copy-start(pred[16,16]{0,1:T(8,128)(4,1)} %constant.15.clone) | copy-start | bytes 772
  218.3 6.9 %copy-start.5 = (s32[16]{0:T(128)S(1)}, s32[16]{0:T(128)}, u32[]{:S(2)}) copy-start(s32[16]{0:T(128)} %copy-done.4) | copy-start | bytes 196
  218.4 9.7 %copy-start.9 = (pred[128,16]{0,1:T(8,128)(4,1)S(1)}, pred[128,16]{0,1:T(8,128)(4,1)}, u32[]{:S(2)}) copy-start(pred[128,16]{0,1:T(8,128)(4,1)} %constant.17.clone) | copy-start | bytes 6148
  232.5 2.0 copy-start.1
Sparse Core Ops, SparseCore 0:
  20.4 59.6 all-gather.4
  82.6 54.8 all-gather.8
  139.1 205.3 all-gather.6
  346.0 204.3 all-gather.10
where the time goes:
time: 658 us; the launch traced here: 651 us
  waiting for transfers between devices  305 us (46%)
  local copies, waits for them, and re-layouts  177 us (27%)
  matrix products  79.8 us (12%)
  other arithmetic  75.2 us (11%)
  between operations  13.9 us (2%)
    all_gather x1, waiting for transfers between devices, body(): lax.all_gather(global_value, ('grp', 'dev'), axis=0, tiled=True)  202 us
    all_gather x1, waiting for transfers between devices, body(): lax.all_gather(global_key, ('grp', 'dev'), axis=0, tiled=True)  103 us
    convert_element_type x1, other arithmetic, body(): return result.reshape(tok_rows, H * head_width).astype(jnp.bfloat16)  45.3 us
    another operation x6, local copies, waits for them, and re-layouts, picked_rows(): source.reshape(source.shape[0] // dilation, dilation, source.shape[1], so...  43.3 us
    dot_general x2, matrix products, attend(): jnp.einsum('hqk,khe->qhe', weights.astype(jnp.bfloat16), value_part, pref...  35.2 us
    unnamed x26, local copies, waits for them, and re-layouts  31.7 us
    dot_general x2, matrix products, attend(): jnp.einsum('qhe,khe->hqk', query_rows, key_part, preferred_element_type=j...  29.6 us
    reduce_sum x2, other arithmetic, attend(): totals = jnp.sum(weights, axis=2)  28.8 us
  transfers between devices with their start and end apart: 4, of which 2 were waited for; matrix products, arithmetic and copies ran while one was open for 34% of the time, Pallas kernels for 0%

commit v1 on v0

--- a/solution.py
+++ b/solution.py
@@ -112,7 +112,12 @@
         start_state(global_query),
         (
             lax.all_gather(global_key, ("grp", "dev"), axis=0, tiled=True),
-            lax.all_gather(global_value, ("grp", "dev"), axis=0, tiled=True),
+            jnp.concatenate(
+                lax.all_to_all(
+                    jnp.stack([global_value] * lax.axis_size(("grp", "dev"))), ("grp", "dev"), 0, 0
+                ),
+                axis=0,
+            ),
         ),
     )
     group_portion = folder(

time: 658 us -> 495 us (0.75)
  waiting for transfers between devices: 305 us -> 129 us
  starting transfers between devices: 0.59 us -> 12.6 us
    all_gather x1 -> x0, waiting for transfers between devices: 202 us -> none  [body(): lax.all_gather(global_value, ('grp', 'dev'), axis=0, tiled=True)]
    all_gather x1, waiting for transfers between devices: 103 us -> 129 us  [body(): lax.all_gather(global_key, ('grp', 'dev'), axis=0, tiled=True)]
    all_to_all x0 -> x1, starting transfers between devices: none -> 12.1 us  [body(): lax.all_to_all(jnp.stack([global_value] * lax.axis_size(('grp', 'dev'))),...]
  transfers between devices with their start and end apart: 4 -> 4, of which waited for: 2 -> 1; matrix products, arithmetic and copies ran while one was open for 34% -> 45% of each run, Pallas kernels for 0% -> 0%
where the time goes in v1:
time: 495 us; the launch traced here: 490 us
  local copies, waits for them, and re-layouts  179 us (36%)
  waiting for transfers between devices  129 us (26%)
  matrix products  79.6 us (16%)
  other arithmetic  75.2 us (15%)
  between operations  13.9 us (3%)
  starting transfers between devices  12.6 us (3%)
    all_gather x1, waiting for transfers between devices, body(): lax.all_gather(global_key, ('grp', 'dev'), axis=0, tiled=True)  129 us
    convert_element_type x1, other arithmetic, body(): return result.reshape(tok_rows, H * head_width).astype(jnp.bfloat16)  45.3 us
    another operation x6, local copies, waits for them, and re-layouts, picked_rows(): source.reshape(source.shape[0] // dilation, dilation, source.shape[1], so...  43.3 us
    dot_general x2, matrix products, attend(): jnp.einsum('hqk,khe->qhe', weights.astype(jnp.bfloat16), value_part, pref...  34.7 us
    unnamed x26, local copies, waits for them, and re-layouts  31.6 us
    dot_general x2, matrix products, attend(): jnp.einsum('qhe,khe->hqk', query_rows, key_part, preferred_element_type=j...  29.6 us
    reduce_sum x2, other arithmetic, attend(): totals = jnp.sum(weights, axis=2)  28.7 us
    broadcast_in_dim x4, local copies, waits for them, and re-layouts, gap_between(): jnp.where(select_mask[None, :, :, None], summed[:, None], 0.0)  21.5 us
  transfers between devices with their start and end apart: 4, of which 1 were waited for; matrix products, arithmetic and copies ran while one was open for 45% of the time, Pallas kernels for 0%

profile of v1, /device:TPU:1, one launch (start us, length us, event | category | flops | bytes accessed | tf_op | source)
XLA Modules:
  0.0 489.7 jit_solution(1338081896155030058)
XLA Ops:
  6.5 3.6 copy.112
  10.2 2.0 copy-done.2
  12.2 4.6 copy.84
  16.8 3.5 gather_fusion.1
  20.6 3.6 copy.119
  26.1 4.7 copy.89
  30.8 3.5 gather_fusion.4
  34.3 9.1 %copy.93 = bf16[8,128,16,128]{3,0,2,1:T(8,128)(2,1)} copy(bf16[8,128,16,128]{3,2,1,0:T(8,128)(2,1)} %bitcast.208) | data formatting | bytes 8388608 | tf_op jit(solution)/shard_map/reshape;reshape | solution.py:55
  43.4 2.8 gather_fusion.5
  46.2 3.0 stack.2
  49.2 12.1 %all-to-all-start = ((bf16[128,8,16,128]{3,1,2,0:T(8,128)(2,1)}), bf16[128,8,16,128]{3,1,2,0:T(8,128)(2,1)}, u32[]{:S(2)}, u32[]{:S(2)}) async-start(bf16[128,8,16,128]{3,1,2,0:T(8,128)(2,1)} %stack.2), calls=%async_computation | async-start | bytes 8388608 | tf_op jit(solution)/shard_map/all_to_all | solution.py:116
  61.6 9.0 %copy.86 = bf16[8,128,16,128]{3,0,2,1:T(8,128)(2,1)} copy(bf16[8,128,16,128]{3,2,1,0:T(8,128)(2,1)} %bitcast.206) | data formatting | bytes 8388608 | tf_op jit(solution)/shard_map/reshape;reshape | solution.py:55
  70.6 3.4 gather_fusion.3
  74.1 6.4 %copy.76 = bf16[1024,2048]{0,1:T(8,128)(2,1)} copy(bf16[1024,2048]{1,0:T(8,128)(2,1)} %param.32) | data formatting | bytes 8388608 | tf_op args[1]
  80.5 6.4 %copy.77 = bf16[1024,2048]{0,1:T(8,128)(2,1)} copy(bf16[1024,2048]{1,0:T(8,128)(2,1)} %param.33) | data formatting | bytes 8388608 | tf_op args[2]
  86.9 5.6 %copy.108 = bf16[128,8,16,128]{3,2,1,0:T(8,128)(2,1)} copy(bf16[128,8,16,128]{3,1,2,0:T(8,128)(2,1)} %bitcast.223) | data formatting | bytes 8388608
  92.5 6.4 %copy.79 = bf16[1024,16,128]{2,0,1:T(8,128)(2,1)} copy(bf16[1024,16,128]{0,2,1:T(8,128)(2,1)} %bitcast.218) | data formatting | bytes 8388608 | tf_op jit(solution)/shard_map/while | solution.py:96
  98.9 6.4 %copy.80 = bf16[1024,16,128]{2,0,1:T(8,128)(2,1)} copy(bf16[1024,16,128]{0,2,1:T(8,128)(2,1)} %bitcast.217) | data formatting | bytes 8388608 | tf_op jit(solution)/shard_map/while | solution.py:96
  105.3 114.6 %while.14 = (s32[]{:T(128)}, f32[2,512,16]{1,0,2:T(2,128)S(1)}, f32[2,512,16]{1,0,2:T(2,128)S(1)}, f32[2,512,16,128]{3,2,1,0:T(8,128)}, bf16[2,512,16,128]{3,2,1...) while((s32[]{:T(128)}, f32[2,512,16]{1,0,2:T(2,128)S(1)}, ...), condition=%wide.region_3.4_spmd, body=%wide.region_0.3_spmd.sunk | while | flops 4362059776 | bytes 145096848 | solution.py:96
  105.8 3.4 constant_dynamic-slice_fusion.2
  109.2 14.7 %multiply_reduce_fusion.3 = (f32[16,512]{1,0:T(8,128)S(1)}, f32[16,512,1024]{2,1,0:T(8,128)}) fusion(bf16[1024,16,128]{2,0,1:T(8,128)(2,1)S(1)} %copy-done, bf16[1,512,16,128]{3,2,1,0:T(8,128)(2,1)} %constant_dynamic-slice_fusion.2), kind=kOutput, calls=%fused_computation.7.clone.1 | convolution fusion | flops 2164252672 | bytes 39878656 | tf_op jit(solution)/shard_map/while/body/eval_jaxpr/qhe,khe->hqk/dot_general | solution.py:14
  124.2 14.4 %fusion.67 = f32[16,512]{1,0:T(8,128)S(1)} fusion(f32[16,512,1024]{2,1,0:T(8,128)} %get-tuple-element.142, f32[16,512]{1,0:T(8,128)S(1)} %get-tuple-element.141), kind=kLoop, calls=%fused_computation.9.clone.1 | loop fusion | flops 25157632 | bytes 33619968 | tf_op jit(solution)/shard_map/while/body/eval_jaxpr/reduce_sum | solution.py:19
  138.8 17.3 %fusion.68 = f32[1,512,16,128]{3,1,2,0:T(8,128)} fusion(bf16[1024,16,128]{2,0,1:T(8,128)(2,1)} %get-tuple-element.167, f32[16,512,1024]{2,1,0:T(8,128)} %get-tuple-element.142, f32[16,512]{1,0:T(8,128)S(1)} %get-tuple-element.141), kind=kOutput, calls=%fused_computation.14.clone.1 | convolution fusion | flops 2172649472 | bytes 41975808 | tf_op jit(solution)/shard_map/while/body/eval_jaxpr/hqk,khe->qhe/dot_general | solution.py:20
  156.1 6.7 %copy_dynamic-update-slice_fusion.2 = f32[2,512,16,128]{3,2,1,0:T(8,128)} fusion(f32[2,512,16,128]{3,2,1,0:T(8,128)} %get-tuple-element.155, s32[]{:T(128)S(6)} %copy.194, f32[1,512,16,128]{3,1,2,0:T(8,128)} %fusion.68), kind=kLoop, calls=%fused_computation.13.clone.1 | loop fusion | bytes 8388612 | tf_op jit(solution)/shard_map/while/body/jit(dynamic_update_index_in_dim)/dynamic_update_slice | solution.py:96
  162.8 3.4 constant_dynamic-slice_fusion.2
  166.2 14.9 %multiply_reduce_fusion.3 = (f32[16,512]{1,0:T(8,128)S(1)}, f32[16,512,1024]{2,1,0:T(8,128)}) fusion(bf16[1024,16,128]{2,0,1:T(8,128)(2,1)S(1)} %copy-done, bf16[1,512,16,128]{3,2,1,0:T(8,128)(2,1)} %constant_dynamic-slice_fusion.2), kind=kOutput, calls=%fused_computation.7.clone.1 | convolution fusion | flops 2164252672 | bytes 39878656 | tf_op jit(solution)/shard_map/while/body/eval_jaxpr/qhe,khe->hqk/dot_general | solution.py:14
  181.3 14.3 %fusion.67 = f32[16,512]{1,0:T(8,128)S(1)} fusion(f32[16,512,1024]{2,1,0:T(8,128)} %get-tuple-element.142, f32[16,512]{1,0:T(8,128)S(1)} %get-tuple-element.141), kind=kLoop, calls=%fused_computation.9.clone.1 | loop fusion | flops 25157632 | bytes 33619968 | tf_op jit(solution)/shard_map/while/body/eval_jaxpr/reduce_sum | solution.py:19
  195.8 17.4 %fusion.68 = f32[1,512,16,128]{3,1,2,0:T(8,128)} fusion(bf16[1024,16,128]{2,0,1:T(8,128)(2,1)} %get-tuple-element.167, f32[16,512,1024]{2,1,0:T(8,128)} %get-tuple-element.142, f32[16,512]{1,0:T(8,128)S(1)} %get-tuple-element.141), kind=kOutput, calls=%fused_computation.14.clone.1 | convolution fusion | flops 2172649472 | bytes 41975808 | tf_op jit(solution)/shard_map/while/body/eval_jaxpr/hqk,khe->qhe/dot_general | solution.py:20
  213.2 6.6 %copy_dynamic-update-slice_fusion.2 = f32[2,512,16,128]{3,2,1,0:T(8,128)} fusion(f32[2,512,16,128]{3,2,1,0:T(8,128)} %get-tuple-element.155, s32[]{:T(128)S(6)} %copy.194, f32[1,512,16,128]{3,1,2,0:T(8,128)} %fusion.68), kind=kLoop, calls=%fused_computation.13.clone.1 | loop fusion | bytes 8388612 | tf_op jit(solution)/shard_map/while/body/jit(dynamic_update_index_in_dim)/dynamic_update_slice | solution.py:96
  220.0 9.0 %copy.85 = bf16[8,128,16,128]{3,0,2,1:T(8,128)(2,1)} copy(bf16[8,128,16,128]{3,2,1,0:T(8,128)(2,1)} %bitcast.203) | data formatting | bytes 8388608 | tf_op jit(solution)/shard_map/reshape;reshape | solution.py:55
  229.0 2.8 gather_fusion.2
  232.2 6.9 %copy.83 = bf16[64,16,16,128]{3,0,2,1:T(8,128)(2,1)} copy(bf16[64,16,16,128]{3,2,1,0:T(8,128)(2,1)} %bitcast.204) | data formatting | bytes 8388608 | tf_op jit(solution)/shard_map/reshape;reshape | solution.py:55
  239.0 2.8 gather_fusion
  242.5 3.8 multiply_reduce_fusion.1
  246.4 2.0 copy-done.1
  250.2 4.8 fusion.26
  255.4 128.8 %all-gather.6.cloned.1.call-done = bf16[1024,16,128]{2,0,1:T(8,128)(2,1)} async-done(((bf16[8,16,128]{2,0,1:T(8,128)(2,1)}), bf16[1024,16,128]{2,0,1:T(8,128)(2,1)}) %all-gather.6.cloned.1.call-update) | async-done | bytes 4194320 | tf_op jit(solution)/shard_map/all_gather | solution.py:114
  384.2 3.4 fusion.53
  388.6 3.1 fusion.32
  392.2 5.9 %div.11 = f32[1024,16,128]{2,1,0:T(8,128)} broadcast(f32[1024,16]{1,0:T(8,128)S(1)} %copy.98), dimensions={0,1} | broadcast | bytes 8454144 | tf_op jit(solution)/shard_map/div | solution.py:82
  398.1 6.0 %mul.91 = f32[1024,16,128]{2,1,0:T(8,128)} broadcast(f32[1024,16]{1,0:T(8,128)S(1)} %copy.96), dimensions={0,1} | broadcast | bytes 8454144 | tf_op jit(solution)/shard_map/mul | solution.py:81
  404.1 3.8 broadcast_in_dim.234
  407.9 6.0 %mul.87 = f32[1024,16,128]{2,1,0:T(8,128)} broadcast(f32[1024,16]{1,0:T(8,128)S(1)} %copy.91), dimensions={0,1} | broadcast | bytes 8454144 | tf_op jit(solution)/shard_map/mul | solution.py:81
  413.9 3.9 broadcast_in_dim.225
  417.8 5.8 %mul.83 = f32[1024,16,128]{2,1,0:T(8,128)} broadcast(f32[1024,16]{1,0:T(8,128)S(1)} %copy.87), dimensions={0,1} | broadcast | bytes 8454144 | tf_op jit(solution)/shard_map/mul | solution.py:81
  423.6 6.9 %broadcast_in_dim.228 = pred[1024,16,128]{2,1,0:T(8,128)(4,1)S(1)} broadcast(pred[1024,16]{1,0:T(8,128)(4,1)S(1)} %copy.92), dimensions={0,1} | broadcast | bytes 2113536 | tf_op jit(solution)/shard_map/jit(_where)/broadcast_in_dim | solution.py:66
  430.5 6.9 %broadcast_in_dim.219 = pred[1024,16,128]{2,1,0:T(8,128)(4,1)S(1)} broadcast(pred[1024,16]{1,0:T(8,128)(4,1)S(1)} %copy.88), dimensions={0,1} | broadcast | bytes 2113536 | tf_op jit(solution)/shard_map/jit(_where)/broadcast_in_dim | solution.py:66
  437.4 45.3 %fusion.11 = bf16[1024,2048]{1,0:T(8,128)(2,1)} fusion(f32[128,8,16,128]{3,2,1,0:T(8,128)} %bitcast.209, f32[128,8,16,128]{3,2,1,0:T(8,128)} %bitcast.210, f32[128,8,16,128]{3,2,1,0:T(8,128)} %bitcast.211, f32[128,8,16,128]{3,2,1,0:T(8,128)} %bitcast.212, f32[128,8,16,128]{3,2,1,0:T(8,128)} %bitcast.213, f32[128,8,16,128]{3,2,1,0:T(8,128)} %bitcast.214, ...), kind=kLoop, calls=%fused_computation.20 | loop fusion | flops 18874368 | bytes 67108864 | tf_op jit(solution)/shard_map/convert_element_type | solution.py:138
  (67 shorter events, 7.8 us)
Async XLA Ops:
  6.5 236.0 %all-gather.4.cloned.1.call-start = ((), (), s32[]{:S(2)}) async-start(), calls=%async_computation.1 | async-start | bytes 4456448 | tf_op jit(solution)/shard_map/all_gather | solution.py:127
  6.5 24.2 %copy-start.4 = (s32[16]{0:T(128)}, s32[16]{0:T(128)S(1)}, u32[]{:S(2)}) copy-start(s32[16]{0:T(128)S(1)} %fusion.48) | copy-start | bytes 196
  10.1 2.0 copy-start.2
  20.3 229.9 %all-gather.8.cloned.1.call-start = ((), (), s32[]{:S(2)}) async-start(), calls=%async_computation.3 | async-start | bytes 4456448 | tf_op jit(solution)/shard_map/all_gather | solution.py:128
  24.2 2.0 copy-start.3
  43.4 27.3 %copy-start.6 = (s32[16]{0:T(128)}, s32[16]{0:T(128)S(1)}, u32[]{:S(2)}) copy-start(s32[16]{0:T(128)S(1)} %fusion.50) | copy-start | bytes 196
  49.2 339.4 %all-to-all-start = ((bf16[128,8,16,128]{3,1,2,0:T(8,128)(2,1)}), bf16[128,8,16,128]{3,1,2,0:T(8,128)(2,1)}, u32[]{:S(2)}, u32[]{:S(2)}) async-start(bf16[128,8,16,128]{3,1,2,0:T(8,128)(2,1)} %stack.2), calls=%async_computation | async-start | bytes 8388608 | tf_op jit(solution)/shard_map/all_to_all | solution.py:116
  61.3 322.9 %all-gather.6.cloned.1.call-start = ((), (), s32[]{:S(2)}) async-start(), calls=%async_computation.2 | async-start | bytes 4227072 | tf_op jit(solution)/shard_map/all_gather | solution.py:114
  105.8 3.5 copy-start
  162.8 3.4 copy-start
  219.9 9.0 %copy-start.7 = (s32[16]{0:T(128)S(1)}, s32[16]{0:T(128)}, u32[]{:S(2)}) copy-start(s32[16]{0:T(128)} %copy-done.6) | copy-start | bytes 196
  219.9 11.8 %copy-start.8 = (pred[16,16]{0,1:T(8,128)(4,1)S(1)}, pred[16,16]{0,1:T(8,128)(4,1)}, u32[]{:S(2)}) copy-start(pred[16,16]{0,1:T(8,128)(4,1)} %constant.15.clone) | copy-start | bytes 772
  232.2 6.9 %copy-start.5 = (s32[16]{0:T(128)S(1)}, s32[16]{0:T(128)}, u32[]{:S(2)}) copy-start(s32[16]{0:T(128)} %copy-done.4) | copy-start | bytes 196
  232.2 9.7 %copy-start.9 = (pred[128,16]{0,1:T(8,128)(4,1)S(1)}, pred[128,16]{0,1:T(8,128)(4,1)}, u32[]{:S(2)}) copy-start(pred[128,16]{0,1:T(8,128)(4,1)} %constant.17.clone) | copy-start | bytes 6148
  246.4 2.0 copy-start.1
Sparse Core Ops, SparseCore 0:
  20.4 96.9 all-gather.3
  119.9 57.2 all-gather.7
  178.8 205.3 all-gather.5
